TPU v7x, 32 devices: a whole 2x2x4 slice. The times are simulated.
32 devices in a mesh: dp: 4 (over z), ctx: 8 (over y, x, core).
Axes of the slice: x: 2, y: 2, z: 4, core: 2. Of those that a mesh axis runs over, the one named last changes fastest.
Arguments:
- tokens: bfloat16 [4, 1024, 8192], P('dp', 'ctx'), may hold values from -6 to 6
- w_down: bfloat16 [8192, 512], P(('dp', 'ctx')), may hold values from -0.0625 to 0.0625
- w_up: bfloat16 [512, 1024], replicated, may hold values from -0.25 to 0.25
- queries: bfloat16 [4, 1024, 4096], P('dp', 'ctx'), may hold values from -70 to 70, as said below
- block_order: int32 [4, 16], P('dp', 'ctx'), may hold values from 0 to 15, each once within a row
Outputs:
- attended: bfloat16 [4, 1024, 4096], P('dp', 'ctx')
Inputs may be any that keep to these rules, and one draw needn't show every extreme that they name: `queries`: query entries.
All inputs are finite; a program needn't handle non-finite values.
Results may differ from a plain program's by a relative error of at most 0.014.
The roundings to bfloat16 on the way count: a program that leaves them out, or rounds other values in their place, can miss the bound.
Values may be sent and summed in bfloat16 or wider, within the bound.
A program may use at most 64 MiB of HBM per device.

v0:
```python
import math
import jax
import jax.numpy as jnp
from jax import lax
from jax.sharding import PartitionSpec as P

QH = 32
KVH = 4
HD = 128


def per_device(tokens, w_down, w_up, queries, block_order):
    local_rows = tokens.shape[1]
    half_rows = local_rows // 2
    features = tokens[0]
    summed = jnp.dot(
        features,
        lax.all_gather(w_down, ("dp", "ctx"), axis=0, tiled=True),
        preferred_element_type=jnp.float32,
    )
    latent = summed.astype(jnp.bfloat16)
    order_whole = lax.all_gather(block_order, "ctx", axis=1, tiled=True)[0]
    block_count = order_whole.shape[0]
    local_ids = jnp.arange(local_rows, dtype=jnp.int32)
    query_pos = (
        jnp.where(local_ids < half_rows, block_order[0, 0], block_order[0, 1]) * half_rows
        + local_ids % half_rows
    )
    group = QH // KVH
    query_heads = queries[0].reshape(local_rows, KVH, group, HD).transpose(1, 2, 0, 3)
    score_scale = HD ** (-0.5)

    def update(carry, kv_block, key_pos):
        running_max, running_total, running_sum = carry
        width = kv_block.shape[0]
        key_block = kv_block[:, : KVH * HD].reshape(width, KVH, HD)
        value_block = kv_block[:, KVH * HD :].reshape(width, KVH, HD)
        scores = (
            jnp.einsum("kgsd,tkd->kgst", query_heads, key_block, preferred_element_type=jnp.float32)
            * score_scale
        )
        allowed = key_pos[None, :] <= query_pos[:, None]
        scores = jnp.where(allowed, scores, -1e30)
        new_max = jnp.maximum(running_max, jnp.max(scores, axis=-1))
        correction = jnp.exp(running_max - new_max)
        expo = jnp.where(allowed, jnp.exp(scores - new_max[..., None]), 0.0)
        new_total = running_total * correction + jnp.sum(expo, axis=-1)
        contrib = jnp.einsum(
            "kgst,tkd->kgsd",
            expo.astype(jnp.bfloat16),
            value_block,
            preferred_element_type=jnp.float32,
        )
        return (new_max, new_total, running_sum * correction[..., None] + contrib)

    start_state = (
        jnp.full((KVH, group, local_rows), -1e30, jnp.float32),
        jnp.zeros((KVH, group, local_rows), jnp.float32),
        jnp.zeros((KVH, group, local_rows, HD), jnp.float32),
    )
    kv_local = jnp.dot(latent, w_up, preferred_element_type=jnp.float32).astype(jnp.bfloat16)
    piece = lax.all_gather(kv_local, "ctx", axis=0, tiled=True)
    count = piece.shape[0]
    width = math.gcd(count, 256)
    blocks = piece.reshape(count // width, width, piece.shape[1])
    row_ids = jnp.arange(count, dtype=jnp.int32)
    onehot = (row_ids // half_rows)[:, None] == jnp.arange(block_count, dtype=jnp.int32)[None, :]
    block_ids = jnp.sum(jnp.where(onehot, order_whole[None, :], 0), axis=1)
    key_positions = (block_ids * half_rows + row_ids % half_rows).reshape(count // width, width)

    def step_block(state, inputs):
        block, key_pos = inputs
        state = update(state, block, key_pos)
        return (state, None)

    result, unused = lax.scan(step_block, start_state, (blocks, key_positions))
    unused_max, final_total, final_sum = result
    outputs = final_sum / final_total[..., None]
    return outputs.transpose(2, 0, 1, 3).reshape(1, local_rows, QH * HD).astype(jnp.bfloat16)


def solution(mesh):
    placed = (
        P("dp", "ctx", None),
        P(("dp", "ctx"), None),
        P(),
        P("dp", "ctx", None),
        P("dp", "ctx"),
    )
    return jax.shard_map(
        per_device, mesh=mesh, in_specs=placed, out_specs=P("dp", "ctx", None), check_vma=False
    )
```

profile of v0, /device:TPU:0, one launch (start us, length us, event | category | flops | bytes accessed | tf_op | source)
XLA Modules:
  0.0 171.8 jit_solution(13662498133776428902)
XLA Ops:
  6.5 0.0 copy-start
  6.5 0.0 all-gather.3.cloned.1.call-start
  6.5 0.7 all-gather.3.cloned.1.call-update
  7.3 0.0 copy-start.4
  7.3 0.0 copy-start.3
  7.3 0.0 all-gather.5.cloned.1.call-start
  7.3 83.1 %all-gather.3.cloned.1.call-done = bf16[8192,512]{1,0:T(8,128)(2,1)} async-done(((bf16[256,512]{1,0:T(8,128)(2,1)}), bf16[8192,512]{1,0:T(8,128)(2,1)}) %all-gather.3.cloned.1.call-update) | async-done | bytes 8388624 | tf_op jit(solution)/shard_map/all_gather | solution.py:18
  90.4 0.0 copy-done
  90.4 5.8 %convolution_convert_fusion = bf16[128,1024]{1,0:T(8,128)(2,1)} fusion(bf16[512,1024]{1,0:T(8,128)(2,1)} %param.9, bf16[8192,512]{1,0:T(8,128)(2,1)} %all-gather.3.cloned.1.call-done, bf16[1,128,8192]{2,1,0:T(8,128)(2,1)S(1)} %copy-done), kind=kOutput, calls=%fused_computation.31 | convolution fusion | flops 1208156160 | bytes 11796480 | tf_op jit(solution)/shard_map/dot_general | solution.py:61
  96.3 0.0 all-gather.5.cloned.1.call-update
  96.3 0.0 copy-done.4
  96.3 0.6 dynamic-slice
  97.5 0.0 copy-done.3
  97.6 0.1 bitcast_dynamic-update-slice_fusion
  97.7 7.3 %all-reduce = s32[16]{0:T(128)S(1)} all-reduce(s32[16]{0:T(128)S(1)} %bitcast_dynamic-update-slice_fusion), channel_id=1, replica_groups=mesh['dp'=4,'ctx'=8] {'ctx'}, use_global_device_ids=true, to_apply=%add | all-reduce | flops 16 | bytes 128
  105.0 0.1 select_reduce_fusion
  105.1 1.6 copy.18
  106.7 1.3 copy.20
  108.0 0.6 fusion.35
  108.7 14.3 %all-gather.5.cloned.1.call-done = bf16[1024,1024]{1,0:T(8,128)(2,1)} async-done(((bf16[128,1024]{1,0:T(8,128)(2,1)}), bf16[1024,1024]{1,0:T(8,128)(2,1)}) %all-gather.5.cloned.1.call-update) | async-done | bytes 2097168 | tf_op jit(solution)/shard_map/all_gather | solution.py:62
  122.9 38.1 %while.15 = (s32[]{:T(128)}, f32[4,8,128]{2,1,0:T(8,128)S(1)}, f32[4,8,128]{2,1,0:T(8,128)S(1)}, f32[4,8,128,128]{3,2,1,0:T(8,128)}, s32[4,256]{1,0:T(4,128)S(1)...) while((s32[]{:T(128)}, f32[4,8,128]{2,1,0:T(8,128)S(1)}, ...), condition=%wide.region_4.5_spmd.clone, body=%wide.region_1.4_spmd.clone.sunk | while | flops 552129792 | bytes 38670536 | solution.py:76
  122.9 1.3 fusion.55
  124.2 0.1 broadcast_compare_fusion.2
  124.3 1.1 constant_dynamic-slice_fusion.5
  125.4 0.2 copy.31
  125.7 0.0 copy-start.1
  125.7 2.2 %fusion.57 = (f32[4,8,128]{2,1,0:T(8,128)S(1)}, f32[4,256,8,128]{3,1,2,0:T(8,128)S(1)}) fusion(pred[128,256]{0,1:T(8,128)(4,1)S(1)} %broadcast_compare_fusion.2, bf16[256,4,128,1]{0,2,3,1:T(8,128)(2,1)S(1)} %bitcast.71, bf16[4,8,128,128]{3,2,1,0:T(8,128)(2,1)} %get-tuple-element.223), kind=kOutput, calls=%fused_computation.3.clone.1 | convolution fusion | flops 271577088 | bytes 5554176 | tf_op jit(solution)/shard_map/while/body/eval_jaxpr/kgsd,tkd->kgst/dot_general | solution.py:39
  127.9 1.1 fusion.58
  129.0 0.0 copy-done.1
  129.0 2.1 %fusion.60 = f32[4,8,128,128]{3,2,1,0:T(8,128)S(1)} fusion(f32[4,8,128,128]{3,2,1,0:T(8,128)S(1)} %copy-done.1, bf16[256,4,128,1]{0,2,3,1:T(8,128)(2,1)S(1)} %bitcast.72, f32[4,256,8,128]{3,1,2,0:T(8,128)S(1)} %get-tuple-element.191, f32[4,8,128]{2,1,0:T(8,128)S(1)} %select_maximum_fusion.2, pred[128,256]{0,1:T(8,128)(4,1)S(1)} %broadcast_compare_fusion.2, ...), kind=kOutput, calls=%fused_computation.8.clone.1 | convolution fusion | flops 275251200 | bytes 8716289 | tf_op jit(solution)/shard_map/while/body/eval_jaxpr/kgst,tkd->kgsd/dot_general | solution.py:48
  131.2 0.0 copy-start.2
  131.2 1.3 copy-done.2
  132.5 1.3 fusion.55
  133.8 0.1 broadcast_compare_fusion.2
  133.9 1.1 constant_dynamic-slice_fusion.5
  135.0 0.2 copy.31
  135.2 0.0 copy-start.1
  135.2 2.2 %fusion.57 = (f32[4,8,128]{2,1,0:T(8,128)S(1)}, f32[4,256,8,128]{3,1,2,0:T(8,128)S(1)}) fusion(pred[128,256]{0,1:T(8,128)(4,1)S(1)} %broadcast_compare_fusion.2, bf16[256,4,128,1]{0,2,3,1:T(8,128)(2,1)S(1)} %bitcast.71, bf16[4,8,128,128]{3,2,1,0:T(8,128)(2,1)} %get-tuple-element.223), kind=kOutput, calls=%fused_computation.3.clone.1 | convolution fusion | flops 271577088 | bytes 5554176 | tf_op jit(solution)/shard_map/while/body/eval_jaxpr/kgsd,tkd->kgst/dot_general | solution.py:39
  137.5 1.1 fusion.58
  138.6 0.0 copy-done.1
  138.6 2.1 %fusion.60 = f32[4,8,128,128]{3,2,1,0:T(8,128)S(1)} fusion(f32[4,8,128,128]{3,2,1,0:T(8,128)S(1)} %copy-done.1, bf16[256,4,128,1]{0,2,3,1:T(8,128)(2,1)S(1)} %bitcast.72, f32[4,256,8,128]{3,1,2,0:T(8,128)S(1)} %get-tuple-element.191, f32[4,8,128]{2,1,0:T(8,128)S(1)} %select_maximum_fusion.2, pred[128,256]{0,1:T(8,128)(4,1)S(1)} %broadcast_compare_fusion.2, ...), kind=kOutput, calls=%fused_computation.8.clone.1 | convolution fusion | flops 275251200 | bytes 8716289 | tf_op jit(solution)/shard_map/while/body/eval_jaxpr/kgst,tkd->kgsd/dot_general | solution.py:48
  140.7 1.3 copy-done.2
  142.0 1.3 fusion.55
  143.3 0.1 broadcast_compare_fusion.2
  143.4 1.1 constant_dynamic-slice_fusion.5
  144.5 0.2 copy.31
  144.7 0.0 copy-start.1
  144.8 2.2 %fusion.57 = (f32[4,8,128]{2,1,0:T(8,128)S(1)}, f32[4,256,8,128]{3,1,2,0:T(8,128)S(1)}) fusion(pred[128,256]{0,1:T(8,128)(4,1)S(1)} %broadcast_compare_fusion.2, bf16[256,4,128,1]{0,2,3,1:T(8,128)(2,1)S(1)} %bitcast.71, bf16[4,8,128,128]{3,2,1,0:T(8,128)(2,1)} %get-tuple-element.223), kind=kOutput, calls=%fused_computation.3.clone.1 | convolution fusion | flops 271577088 | bytes 5554176 | tf_op jit(solution)/shard_map/while/body/eval_jaxpr/kgsd,tkd->kgst/dot_general | solution.py:39
  147.0 1.1 fusion.58
  148.1 2.1 %fusion.60 = f32[4,8,128,128]{3,2,1,0:T(8,128)S(1)} fusion(f32[4,8,128,128]{3,2,1,0:T(8,128)S(1)} %copy-done.1, bf16[256,4,128,1]{0,2,3,1:T(8,128)(2,1)S(1)} %bitcast.72, f32[4,256,8,128]{3,1,2,0:T(8,128)S(1)} %get-tuple-element.191, f32[4,8,128]{2,1,0:T(8,128)S(1)} %select_maximum_fusion.2, pred[128,256]{0,1:T(8,128)(4,1)S(1)} %broadcast_compare_fusion.2, ...), kind=kOutput, calls=%fused_computation.8.clone.1 | convolution fusion | flops 275251200 | bytes 8716289 | tf_op jit(solution)/shard_map/while/body/eval_jaxpr/kgst,tkd->kgsd/dot_general | solution.py:48
  150.2 1.3 copy-done.2
  151.5 1.3 fusion.55
  152.8 0.1 broadcast_compare_fusion.2
  152.9 1.1 constant_dynamic-slice_fusion.5
  154.0 0.2 copy.31
  154.3 2.2 %fusion.57 = (f32[4,8,128]{2,1,0:T(8,128)S(1)}, f32[4,256,8,128]{3,1,2,0:T(8,128)S(1)}) fusion(pred[128,256]{0,1:T(8,128)(4,1)S(1)} %broadcast_compare_fusion.2, bf16[256,4,128,1]{0,2,3,1:T(8,128)(2,1)S(1)} %bitcast.71, bf16[4,8,128,128]{3,2,1,0:T(8,128)(2,1)} %get-tuple-element.223), kind=kOutput, calls=%fused_computation.3.clone.1 | convolution fusion | flops 271577088 | bytes 5554176 | tf_op jit(solution)/shard_map/while/body/eval_jaxpr/kgsd,tkd->kgst/dot_general | solution.py:39
  156.5 1.1 fusion.58
  157.6 0.0 copy-done.1
  157.6 2.1 %fusion.60 = f32[4,8,128,128]{3,2,1,0:T(8,128)S(1)} fusion(f32[4,8,128,128]{3,2,1,0:T(8,128)S(1)} %copy-done.1, bf16[256,4,128,1]{0,2,3,1:T(8,128)(2,1)S(1)} %bitcast.72, f32[4,256,8,128]{3,1,2,0:T(8,128)S(1)} %get-tuple-element.191, f32[4,8,128]{2,1,0:T(8,128)S(1)} %select_maximum_fusion.2, pred[128,256]{0,1:T(8,128)(4,1)S(1)} %broadcast_compare_fusion.2, ...), kind=kOutput, calls=%fused_computation.8.clone.1 | convolution fusion | flops 275251200 | bytes 8716289 | tf_op jit(solution)/shard_map/while/body/eval_jaxpr/kgst,tkd->kgsd/dot_general | solution.py:48
  159.7 0.0 copy-start.2
  159.7 1.3 copy-done.2
  161.0 1.9 %fusion.28 = bf16[128,4,8,128]{3,0,2,1:T(8,128)(2,1)S(1)} fusion(f32[4,8,128,128]{3,2,1,0:T(8,128)} %get-tuple-element.48, f32[4,8,128]{2,1,0:T(8,128)S(1)} %get-tuple-element.49), kind=kLoop, calls=%fused_computation.33 | loop fusion | flops 1048576 | bytes 3162112 | tf_op jit(solution)/shard_map/convert_element_type | solution.py:79
  163.0 0.7 copy.21
  163.7 1.3 convert_element_type.30
  (32 shorter events, 0.3 us)
Async XLA Ops:
  6.5 83.9 %copy-start = (bf16[1,128,8192]{2,1,0:T(8,128)(2,1)S(1)}, bf16[1,128,8192]{2,1,0:T(8,128)(2,1)}, u32[]{:S(2)}) copy-start(bf16[1,128,8192]{2,1,0:T(8,128)(2,1)} %param.7) | copy-start | bytes 6291460
  6.5 83.9 %all-gather.3.cloned.1.call-start = ((), (), s32[]{:S(2)}) async-start(), calls=%async_computation | async-start | bytes 8650752 | tf_op jit(solution)/shard_map/all_gather | solution.py:18
  7.3 89.0 %copy-start.4 = (u32[32]{0:T(128)S(1)}, u32[32]{0:T(128)}, u32[]{:S(2)}) copy-start(u32[32]{0:T(128)} %constant.71) | copy-start | bytes 388
  7.3 90.3 %copy-start.3 = (s32[1,2]{1,0:T(1,128)S(1)}, s32[1,2]{1,0:T(1,128)}, u32[]{:S(2)}) copy-start(s32[1,2]{1,0:T(1,128)} %param.11) | copy-start | bytes 28
  7.3 115.6 %all-gather.5.cloned.1.call-start = ((), (), s32[]{:S(2)}) async-start(), calls=%async_computation.1 | async-start | bytes 2359296 | tf_op jit(solution)/shard_map/all_gather | solution.py:62
  125.7 3.3 %copy-start.1 = (f32[4,8,128,128]{3,2,1,0:T(8,128)S(1)}, f32[4,8,128,128]{3,2,1,0:T(8,128)}, u32[]{:S(2)}) copy-start(f32[4,8,128,128]{3,2,1,0:T(8,128)} %get-tuple-element.209) | copy-start | bytes 6291460 | tf_op jit(solution)/shard_map/while
  131.2 1.3 copy-start.2
  135.2 3.3 %copy-start.1 = (f32[4,8,128,128]{3,2,1,0:T(8,128)S(1)}, f32[4,8,128,128]{3,2,1,0:T(8,128)}, u32[]{:S(2)}) copy-start(f32[4,8,128,128]{3,2,1,0:T(8,128)} %get-tuple-element.209) | copy-start | bytes 6291460 | tf_op jit(solution)/shard_map/while
  140.7 1.3 copy-start.2
  144.7 3.3 %copy-start.1 = (f32[4,8,128,128]{3,2,1,0:T(8,128)S(1)}, f32[4,8,128,128]{3,2,1,0:T(8,128)}, u32[]{:S(2)}) copy-start(f32[4,8,128,128]{3,2,1,0:T(8,128)} %get-tuple-element.209) | copy-start | bytes 6291460 | tf_op jit(solution)/shard_map/while
  150.2 1.3 copy-start.2
  154.3 3.3 %copy-start.1 = (f32[4,8,128,128]{3,2,1,0:T(8,128)S(1)}, f32[4,8,128,128]{3,2,1,0:T(8,128)}, u32[]{:S(2)}) copy-start(f32[4,8,128,128]{3,2,1,0:T(8,128)} %get-tuple-element.209) | copy-start | bytes 6291460 | tf_op jit(solution)/shard_map/while
  159.7 1.3 copy-start.2
Sparse Core Ops, SparseCore 0:
  10.2 80.1 all-gather.2
  96.4 26.4 all-gather.4
where the time goes:
time: 172 us
  waiting for transfers between devices  98.1 us (57%)
  matrix products  23.1 us (13%)
  local copies, waits for them, and re-layouts  16.7 us (10%)
  between operations  14.1 us (8%)
  other arithmetic  12 us (7%)
  blocking collectives  7.34 us (4%)
    all_gather x1, waiting for transfers between devices, per_device(): lax.all_gather(w_down, ('dp', 'ctx'), axis=0, tiled=True)  83.1 us
    all_gather x1, waiting for transfers between devices, per_device(): piece = lax.all_gather(kv_local, 'ctx', axis=0, tiled=True)  14.3 us
    dot_general x4, matrix products, update(): jnp.einsum('kgsd,tkd->kgst', query_heads, key_block, preferred_element_ty...  8.83 us
    dot_general x4, matrix products, update(): jnp.einsum('kgst,tkd->kgsd', expo.astype(jnp.bfloat16), value_block, pref...  8.43 us
    unnamed x1, blocking collectives  7.34 us
    dot_general x1, matrix products, per_device(): jnp.dot(latent, w_up, preferred_element_type=jnp.float32)  5.84 us
    dynamic_slice x12, local copies, waits for them, and re-layouts, per_device(): result, unused = lax.scan(step_block, start_state, (blocks, key_positions))  5.19 us
    while x20, local copies, waits for them, and re-layouts  5.18 us
  transfers between devices with their start and end apart: 2, of which 2 were waited for; matrix products, arithmetic and copies ran while one was open for 3% of the time, Pallas kernels for 0%

commit v1 on v0

--- a/solution.py
+++ b/solution.py
@@ -7,6 +7,18 @@
 QH = 32
 KVH = 4
 HD = 128
+
+
+def gather_by_bits(x, axis, dim):
+    ways, here, hop = (lax.axis_size(axis), lax.axis_index(axis), x.shape[dim])
+    line, have = (x, 1)
+    while have < ways:
+        line = jnp.concatenate(
+            [line, lax.ppermute(line, axis, [(d, (d - have) % ways) for d in range(ways)])],
+            axis=dim,
+        )
+        have = 2 * have
+    return jnp.roll(line, here * hop, axis=dim)
 
 
 def per_device(tokens, w_down, w_up, queries, block_order):
@@ -59,7 +71,7 @@
         jnp.zeros((KVH, group, local_rows, HD), jnp.float32),
     )
     kv_local = jnp.dot(latent, w_up, preferred_element_type=jnp.float32).astype(jnp.bfloat16)
-    piece = lax.all_gather(kv_local, "ctx", axis=0, tiled=True)
+    piece = gather_by_bits(kv_local, "ctx", 0)
     count = piece.shape[0]
     width = math.gcd(count, 256)
     blocks = piece.reshape(count // width, width, piece.shape[1])

time: 172 us -> 228 us (1.33)
  blocking collectives: 7.34 us -> 23.8 us
  matrix products: 23.1 us -> 36.8 us
  other arithmetic: 12 us -> 23.2 us
  local copies, waits for them, and re-layouts: 16.7 us -> 24.8 us
  starting transfers between devices: 0.04 us -> 4.51 us
    unnamed x1, blocking collectives: 7.34 us -> 23.8 us
    ppermute x0 -> x3, waiting for transfers between devices: none -> 15.8 us  [gather_by_bits(): lax.ppermute(line, axis, [(d, (d - have) % ways) for d in range(ways)])]
    all_gather x1 -> x0, waiting for transfers between devices: 14.3 us -> none  [per_device(): piece = lax.all_gather(kv_local, 'ctx', axis=0, tiled=True)]
    reduce_sum x4, other arithmetic: 4.29 us -> 13.6 us  [update(): new_total = running_total * correction + jnp.sum(expo, axis=-1)]
    unnamed x11 -> x17, local copies, waits for them, and re-layouts: 3.63 us -> 11.4 us
    dot_general x4, matrix products: 8.83 us -> 16 us  [update(): jnp.einsum('kgsd,tkd->kgst', query_heads, key_block, preferred_element_ty...]
    dot_general x4, matrix products: 8.43 us -> 15 us  [update(): jnp.einsum('kgst,tkd->kgsd', expo.astype(jnp.bfloat16), value_block, pref...]
    while x20 -> x12, local copies, waits for them, and re-layouts: 5.18 us -> 0.08 us
  transfers between devices with their start and end apart: 2 -> 4, of which waited for: 2 -> 3; matrix products, arithmetic and copies ran while one was open for 3% -> 3% of each run, Pallas kernels for 0% -> 0%
where the time goes in v1:
time: 228 us; the launch traced here: 227 us
  waiting for transfers between devices  99.7 us (44%)
  matrix products  36.8 us (16%)
  local copies, waits for them, and re-layouts  24.8 us (11%)
  blocking collectives  23.8 us (10%)
  other arithmetic  23.2 us (10%)
  between operations  14.1 us (6%)
  starting transfers between devices  4.51 us (2%)
    all_gather x1, waiting for transfers between devices, per_device(): lax.all_gather(w_down, ('dp', 'ctx'), axis=0, tiled=True)  83.1 us
    unnamed x1, blocking collectives  23.8 us
    dot_general x4, matrix products, update(): jnp.einsum('kgsd,tkd->kgst', query_heads, key_block, preferred_element_ty...  16 us
    ppermute x3, waiting for transfers between devices, gather_by_bits(): lax.ppermute(line, axis, [(d, (d - have) % ways) for d in range(ways)])  15.8 us
    dot_general x4, matrix products, update(): jnp.einsum('kgst,tkd->kgsd', expo.astype(jnp.bfloat16), value_block, pref...  15 us
    reduce_sum x4, other arithmetic, update(): new_total = running_total * correction + jnp.sum(expo, axis=-1)  13.6 us
    unnamed x17, local copies, waits for them, and re-layouts  11.4 us
    dot_general x1, matrix products, per_device(): jnp.dot(latent, w_up, preferred_element_type=jnp.float32)  5.84 us
  transfers between devices with their start and end apart: 4, of which 3 were waited for; matrix products, arithmetic and copies ran while one was open for 3% of the time, Pallas kernels for 0%

profile of v1, /device:TPU:0, one launch (start us, length us, event | category | flops | bytes accessed | tf_op | source)
XLA Modules:
  0.0 227.1 jit_solution(10717955070420918946)
XLA Ops:
  6.5 0.7 all-gather.2.cloned.1.call-update
  7.3 0.0 copy-start.3
  7.3 83.1 %all-gather.2.cloned.1.call-done = bf16[8192,512]{1,0:T(8,128)(2,1)} async-done(((bf16[256,512]{1,0:T(8,128)(2,1)}), bf16[8192,512]{1,0:T(8,128)(2,1)}) %all-gather.2.cloned.1.call-update) | async-done | bytes 8388624 | tf_op jit(solution)/shard_map/all_gather | solution.py:30
  90.4 5.8 %constant_dynamic-update-slice_fusion.7 = (bf16[2048,1024]{1,0:T(8,128)(2,1)}, bf16[128,1024]{1,0:T(8,128)(2,1)S(1)}) fusion(bf16[512,1024]{1,0:T(8,128)(2,1)} %param.9, bf16[8192,512]{1,0:T(8,128)(2,1)} %all-gather.2.cloned.1.call-done, bf16[1,128,8192]{2,1,0:T(8,128)(2,1)S(1)} %copy-done), kind=kOutput, calls=%fused_computation.45 | convolution fusion | flops 1208156160 | bytes 12058624 | tf_op jit(solution)/shard_map/dot_general | solution.py:73
  96.3 1.3 collective-permute-start
  97.6 3.9 %collective-permute-done = bf16[128,1024]{1,0:T(8,128)(2,1)S(1)} collective-permute-done((bf16[128,1024]{1,0:T(8,128)(2,1)S(1)}, bf16[128,1024]{1,0:T(8,128)(2,1)S(1)}, u32[]{:S(2)}, u32[]{:S(2)}) %collective-permute-start) | collective-permute-done | bytes 262176 | tf_op jit(solution)/shard_map/ppermute | solution.py:17
  101.5 0.8 pad_maximum_fusion.1
  102.3 1.5 collective-permute-start.1
  103.8 0.0 copy-done.3
  103.8 0.6 dynamic-slice
  105.0 11.9 %collective-permute-done.1 = bf16[256,1024]{1,0:T(8,128)(2,1)S(1)} collective-permute-done((bf16[256,1024]{1,0:T(8,128)(2,1)}, bf16[256,1024]{1,0:T(8,128)(2,1)S(1)}, u32[]{:S(2)}, u32[]{:S(2)}) %collective-permute-start.1) | collective-permute-done | bytes 524320 | tf_op jit(solution)/shard_map/ppermute | solution.py:17
  117.0 1.0 pad_maximum_fusion
  118.0 1.7 collective-permute-start.2
  119.7 0.1 bitcast_dynamic-update-slice_fusion
  119.8 23.8 %all-reduce = s32[16]{0:T(128)S(1)} all-reduce(s32[16]{0:T(128)S(1)} %bitcast_dynamic-update-slice_fusion), channel_id=1, replica_groups=mesh['dp'=4,'ctx'=8] {'ctx'}, use_global_device_ids=true, to_apply=%add | all-reduce | flops 16 | bytes 128
  143.6 0.1 select_reduce_fusion
  143.7 2.3 %copy.24 = bf16[1,128,4096]{1,2,0:T(8,128)(2,1)} copy(bf16[1,128,4096]{2,1,0:T(8,128)(2,1)} %param.10) | data formatting | bytes 2097152 | tf_op args[3]
  146.0 2.3 %copy.26 = bf16[4,8,128,128]{3,2,1,0:T(8,128)(2,1)} copy(bf16[4,8,128,128]{2,3,1,0:T(8,128)(2,1)} %bitcast.76) | data formatting | bytes 2097152
  148.3 0.6 fusion.35
  149.0 0.7 constant_dynamic-update-slice_fusion.6
  149.7 0.9 constant_dynamic-update-slice_fusion.5
  150.6 0.0 collective-permute-done.2
  150.6 2.2 constant_dynamic-update-slice_fusion.4
  152.8 0.7 constant_dynamic-update-slice_fusion.3
  153.6 0.7 constant_dynamic-update-slice_fusion.2
  154.3 0.8 constant_dynamic-update-slice_fusion.1
  155.1 2.3 constant_dynamic-update-slice_fusion
  157.4 3.1 %constant_dynamic-slice_fusion.2 = bf16[1024,1024]{1,0:T(8,128)(2,1)} fusion(bf16[2048,1024]{1,0:T(8,128)(2,1)} %constant_dynamic-update-slice_fusion, s32[]{:T(128)S(6)} %select_n.56), kind=kLoop, calls=%fused_computation.60 | loop fusion | bytes 4194308 | tf_op jit(solution)/shard_map/jit(_roll_dynamic)/dynamic_slice | solution.py:21
  160.5 55.8 %while.15 = (s32[]{:T(128)}, f32[4,8,128]{2,1,0:T(8,128)S(1)}, f32[4,8,128]{2,1,0:T(8,128)S(1)}, f32[4,8,128,128]{3,2,1,0:T(8,128)}, s32[4,256]{1,0:T(4,128)S(1)...) while((s32[]{:T(128)}, f32[4,8,128]{2,1,0:T(8,128)S(1)}, ...), condition=%wide.region_4.5_spmd.clone, body=%wide.region_1.4_spmd.clone.sunk | while | flops 552129792 | bytes 38670500 | solution.py:88
  160.5 1.3 fusion.57
  161.8 0.1 broadcast_compare_fusion.2
  161.9 1.1 constant_dynamic-slice_fusion.6
  163.0 0.2 copy.37
  163.2 4.0 %fusion.59 = (f32[4,8,128]{2,1,0:T(8,128)S(1)}, f32[4,256,8,128]{3,1,2,0:T(8,128)}) fusion(pred[128,256]{0,1:T(8,128)(4,1)S(1)} %broadcast_compare_fusion.2, bf16[256,4,128,1]{0,2,3,1:T(8,128)(2,1)S(1)} %bitcast.73, bf16[4,8,128,128]{3,2,1,0:T(8,128)(2,1)} %get-tuple-element.234), kind=kOutput, calls=%fused_computation.3.clone.1 | convolution fusion | flops 271577088 | bytes 5554176 | tf_op jit(solution)/shard_map/while/body/eval_jaxpr/kgsd,tkd->kgst/dot_general | solution.py:51
  167.2 3.4 %fusion.60 = f32[4,8,128]{2,1,0:T(8,128)S(1)} fusion(f32[4,256,8,128]{3,1,2,0:T(8,128)} %get-tuple-element.202, f32[4,8,128]{2,1,0:T(8,128)S(1)} %select_maximum_fusion.2, pred[128,256]{0,1:T(8,128)(4,1)S(1)} %broadcast_compare_fusion.2), kind=kLoop, calls=%fused_computation.5.clone.1 | loop fusion | flops 5238784 | bytes 4259840 | tf_op jit(solution)/shard_map/while/body/eval_jaxpr/reduce_sum | solution.py:59
  170.7 0.0 copy-done.1
  170.7 2.9 %fusion.62 = f32[4,8,128,128]{3,2,1,0:T(8,128)} fusion(f32[4,8,128,128]{3,2,1,0:T(8,128)} %get-tuple-element.220, bf16[256,4,128,1]{0,2,3,1:T(8,128)(2,1)S(1)} %bitcast.75, f32[4,256,8,128]{3,1,2,0:T(8,128)S(1)} %copy-done.1, f32[4,8,128]{2,1,0:T(8,128)S(1)} %select_maximum_fusion.2, pred[128,256]{0,1:T(8,128)(4,1)S(1)} %broadcast_compare_fusion.2, ...), kind=kOutput, calls=%fused_computation.8.clone.1 | convolution fusion | flops 275251200 | bytes 8716289 | tf_op jit(solution)/shard_map/while/body/eval_jaxpr/kgst,tkd->kgsd/dot_general | solution.py:60
  173.5 1.3 fusion.57
  174.9 0.1 broadcast_compare_fusion.2
  175.0 1.1 constant_dynamic-slice_fusion.6
  176.1 0.2 copy.37
  176.3 4.0 %fusion.59 = (f32[4,8,128]{2,1,0:T(8,128)S(1)}, f32[4,256,8,128]{3,1,2,0:T(8,128)}) fusion(pred[128,256]{0,1:T(8,128)(4,1)S(1)} %broadcast_compare_fusion.2, bf16[256,4,128,1]{0,2,3,1:T(8,128)(2,1)S(1)} %bitcast.73, bf16[4,8,128,128]{3,2,1,0:T(8,128)(2,1)} %get-tuple-element.234), kind=kOutput, calls=%fused_computation.3.clone.1 | convolution fusion | flops 271577088 | bytes 5554176 | tf_op jit(solution)/shard_map/while/body/eval_jaxpr/kgsd,tkd->kgst/dot_general | solution.py:51
  180.3 3.4 %fusion.60 = f32[4,8,128]{2,1,0:T(8,128)S(1)} fusion(f32[4,256,8,128]{3,1,2,0:T(8,128)} %get-tuple-element.202, f32[4,8,128]{2,1,0:T(8,128)S(1)} %select_maximum_fusion.2, pred[128,256]{0,1:T(8,128)(4,1)S(1)} %broadcast_compare_fusion.2), kind=kLoop, calls=%fused_computation.5.clone.1 | loop fusion | flops 5238784 | bytes 4259840 | tf_op jit(solution)/shard_map/while/body/eval_jaxpr/reduce_sum | solution.py:59
  183.7 0.0 copy-done.1
  183.8 4.0 %fusion.62 = f32[4,8,128,128]{3,2,1,0:T(8,128)} fusion(f32[4,8,128,128]{3,2,1,0:T(8,128)} %get-tuple-element.220, bf16[256,4,128,1]{0,2,3,1:T(8,128)(2,1)S(1)} %bitcast.75, f32[4,256,8,128]{3,1,2,0:T(8,128)S(1)} %copy-done.1, f32[4,8,128]{2,1,0:T(8,128)S(1)} %select_maximum_fusion.2, pred[128,256]{0,1:T(8,128)(4,1)S(1)} %broadcast_compare_fusion.2, ...), kind=kOutput, calls=%fused_computation.8.clone.1 | convolution fusion | flops 275251200 | bytes 8716289 | tf_op jit(solution)/shard_map/while/body/eval_jaxpr/kgst,tkd->kgsd/dot_general | solution.py:60
  187.8 1.3 fusion.57
  189.1 0.1 broadcast_compare_fusion.2
  189.2 1.1 constant_dynamic-slice_fusion.6
  190.3 0.2 copy.37
  190.6 4.0 %fusion.59 = (f32[4,8,128]{2,1,0:T(8,128)S(1)}, f32[4,256,8,128]{3,1,2,0:T(8,128)}) fusion(pred[128,256]{0,1:T(8,128)(4,1)S(1)} %broadcast_compare_fusion.2, bf16[256,4,128,1]{0,2,3,1:T(8,128)(2,1)S(1)} %bitcast.73, bf16[4,8,128,128]{3,2,1,0:T(8,128)(2,1)} %get-tuple-element.234), kind=kOutput, calls=%fused_computation.3.clone.1 | convolution fusion | flops 271577088 | bytes 5554176 | tf_op jit(solution)/shard_map/while/body/eval_jaxpr/kgsd,tkd->kgst/dot_general | solution.py:51
  194.6 3.4 %fusion.60 = f32[4,8,128]{2,1,0:T(8,128)S(1)} fusion(f32[4,256,8,128]{3,1,2,0:T(8,128)} %get-tuple-element.202, f32[4,8,128]{2,1,0:T(8,128)S(1)} %select_maximum_fusion.2, pred[128,256]{0,1:T(8,128)(4,1)S(1)} %broadcast_compare_fusion.2), kind=kLoop, calls=%fused_computation.5.clone.1 | loop fusion | flops 5238784 | bytes 4259840 | tf_op jit(solution)/shard_map/while/body/eval_jaxpr/reduce_sum | solution.py:59
  198.0 0.0 copy-done.1
  198.0 4.0 %fusion.62 = f32[4,8,128,128]{3,2,1,0:T(8,128)} fusion(f32[4,8,128,128]{3,2,1,0:T(8,128)} %get-tuple-element.220, bf16[256,4,128,1]{0,2,3,1:T(8,128)(2,1)S(1)} %bitcast.75, f32[4,256,8,128]{3,1,2,0:T(8,128)S(1)} %copy-done.1, f32[4,8,128]{2,1,0:T(8,128)S(1)} %select_maximum_fusion.2, pred[128,256]{0,1:T(8,128)(4,1)S(1)} %broadcast_compare_fusion.2, ...), kind=kOutput, calls=%fused_computation.8.clone.1 | convolution fusion | flops 275251200 | bytes 8716289 | tf_op jit(solution)/shard_map/while/body/eval_jaxpr/kgst,tkd->kgsd/dot_general | solution.py:60
  202.1 1.3 fusion.57
  203.4 0.1 broadcast_compare_fusion.2
  203.5 1.1 constant_dynamic-slice_fusion.6
  204.6 0.2 copy.37
  204.8 4.0 %fusion.59 = (f32[4,8,128]{2,1,0:T(8,128)S(1)}, f32[4,256,8,128]{3,1,2,0:T(8,128)}) fusion(pred[128,256]{0,1:T(8,128)(4,1)S(1)} %broadcast_compare_fusion.2, bf16[256,4,128,1]{0,2,3,1:T(8,128)(2,1)S(1)} %bitcast.73, bf16[4,8,128,128]{3,2,1,0:T(8,128)(2,1)} %get-tuple-element.234), kind=kOutput, calls=%fused_computation.3.clone.1 | convolution fusion | flops 271577088 | bytes 5554176 | tf_op jit(solution)/shard_map/while/body/eval_jaxpr/kgsd,tkd->kgst/dot_general | solution.py:51
  208.8 3.4 %fusion.60 = f32[4,8,128]{2,1,0:T(8,128)S(1)} fusion(f32[4,256,8,128]{3,1,2,0:T(8,128)} %get-tuple-element.202, f32[4,8,128]{2,1,0:T(8,128)S(1)} %select_maximum_fusion.2, pred[128,256]{0,1:T(8,128)(4,1)S(1)} %broadcast_compare_fusion.2), kind=kLoop, calls=%fused_computation.5.clone.1 | loop fusion | flops 5238784 | bytes 4259840 | tf_op jit(solution)/shard_map/while/body/eval_jaxpr/reduce_sum | solution.py:59
  212.2 0.0 copy-done.1
  212.3 4.0 %fusion.62 = f32[4,8,128,128]{3,2,1,0:T(8,128)} fusion(f32[4,8,128,128]{3,2,1,0:T(8,128)} %get-tuple-element.220, bf16[256,4,128,1]{0,2,3,1:T(8,128)(2,1)S(1)} %bitcast.75, f32[4,256,8,128]{3,1,2,0:T(8,128)S(1)} %copy-done.1, f32[4,8,128]{2,1,0:T(8,128)S(1)} %select_maximum_fusion.2, pred[128,256]{0,1:T(8,128)(4,1)S(1)} %broadcast_compare_fusion.2, ...), kind=kOutput, calls=%fused_computation.8.clone.1 | convolution fusion | flops 275251200 | bytes 8716289 | tf_op jit(solution)/shard_map/while/body/eval_jaxpr/kgst,tkd->kgsd/dot_general | solution.py:60
  216.3 1.9 fusion.28
  218.3 0.7 copy.27
  219.0 1.3 convert_element_type.30
  (37 shorter events, 0.3 us)
Async XLA Ops:
  6.5 83.9 %copy-start = (bf16[1,128,8192]{2,1,0:T(8,128)(2,1)S(1)}, bf16[1,128,8192]{2,1,0:T(8,128)(2,1)}, u32[]{:S(2)}) copy-start(bf16[1,128,8192]{2,1,0:T(8,128)(2,1)} %param.7) | copy-start | bytes 6291460
  6.5 83.9 %all-gather.2.cloned.1.call-start = ((), (), s32[]{:S(2)}) async-start(), calls=%async_computation | async-start | bytes 8650752 | tf_op jit(solution)/shard_map/all_gather | solution.py:30
  7.3 96.5 %copy-start.3 = (u32[32]{0:T(128)S(1)}, u32[32]{0:T(128)}, u32[]{:S(2)}) copy-start(u32[32]{0:T(128)} %constant.98) | copy-start | bytes 388
  7.3 112.4 %copy-start.2 = (s32[1,2]{1,0:T(1,128)S(1)}, s32[1,2]{1,0:T(1,128)}, u32[]{:S(2)}) copy-start(s32[1,2]{1,0:T(1,128)} %param.11) | copy-start | bytes 28
  96.3 5.2 %collective-permute-start = (bf16[128,1024]{1,0:T(8,128)(2,1)S(1)}, bf16[128,1024]{1,0:T(8,128)(2,1)S(1)}, u32[]{:S(2)}, u32[]{:S(2)}) collective-permute-start(bf16[128,1024]{1,0:T(8,128)(2,1)S(1)} %get-tuple-element.138), channel_id=1, source_target_pairs={{0,7},{1,0},{2,1},{3,2},{4,3},{5,4},{6,5},{7,6},{8,15},{9,8},{10,9... | collective-permute-start | bytes 786440 | tf_op jit(solution)/shard_map/ppermute | solution.py:17
  102.3 14.6 %collective-permute-start.1 = (bf16[256,1024]{1,0:T(8,128)(2,1)}, bf16[256,1024]{1,0:T(8,128)(2,1)S(1)}, u32[]{:S(2)}, u32[]{:S(2)}) collective-permute-start(bf16[256,1024]{1,0:T(8,128)(2,1)} %pad_maximum_fusion.1), channel_id=1, source_target_pairs={{0,6},{1,7},{2,0},{3,1},{4,2},{5,3},{6,4},{7,5},{8,14},{9,15},{10,... | collective-permute-start | bytes 1572872 | tf_op jit(solution)/shard_map/ppermute | solution.py:17
  118.0 32.6 %collective-permute-start.2 = (bf16[512,1024]{1,0:T(8,128)(2,1)}, bf16[512,1024]{1,0:T(8,128)(2,1)}, u32[]{:S(2)}, u32[]{:S(2)}) collective-permute-start(bf16[512,1024]{1,0:T(8,128)(2,1)} %pad_maximum_fusion), channel_id=1, source_target_pairs={{0,4},{1,5},{2,6},{3,7},{4,0},{5,1},{6,2},{7,3},{8,12},{9,13},{10,... | collective-permute-start | bytes 3145736 | tf_op jit(solution)/shard_map/ppermute | solution.py:17
  167.2 3.4 %copy-start.1 = (f32[4,256,8,128]{3,1,2,0:T(8,128)S(1)}, f32[4,256,8,128]{3,1,2,0:T(8,128)}, u32[]{:S(2)}) copy-start(f32[4,256,8,128]{3,1,2,0:T(8,128)} %get-tuple-element.202) | copy-start | bytes 12582916 | tf_op jit(solution)/shard_map/while
  180.3 3.4 %copy-start.1 = (f32[4,256,8,128]{3,1,2,0:T(8,128)S(1)}, f32[4,256,8,128]{3,1,2,0:T(8,128)}, u32[]{:S(2)}) copy-start(f32[4,256,8,128]{3,1,2,0:T(8,128)} %get-tuple-element.202) | copy-start | bytes 12582916 | tf_op jit(solution)/shard_map/while
  194.6 3.4 %copy-start.1 = (f32[4,256,8,128]{3,1,2,0:T(8,128)S(1)}, f32[4,256,8,128]{3,1,2,0:T(8,128)}, u32[]{:S(2)}) copy-start(f32[4,256,8,128]{3,1,2,0:T(8,128)} %get-tuple-element.202) | copy-start | bytes 12582916 | tf_op jit(solution)/shard_map/while
  208.8 3.4 %copy-start.1 = (f32[4,256,8,128]{3,1,2,0:T(8,128)S(1)}, f32[4,256,8,128]{3,1,2,0:T(8,128)}, u32[]{:S(2)}) copy-start(f32[4,256,8,128]{3,1,2,0:T(8,128)} %get-tuple-element.202) | copy-start | bytes 12582916 | tf_op jit(solution)/shard_map/while
Sparse Core Ops, SparseCore 0:
  10.2 80.1 all-gather.1
